TPU v7x, 32 devices: a whole 2x2x4 slice. The times are simulated.
32 devices in a mesh: section: 4 (over z), ep: 8 (over y, x, core).
Axes of the slice: x: 2, y: 2, z: 4, core: 2. Of those that a mesh axis runs over, the one named last changes fastest.
Arguments:
- flight_a: bfloat16 [4, 1024, 3584], P('section', 'ep'), may hold values from -6 to 6
- flight_b: bfloat16 [4, 1024, 3584], P('section', 'ep'), may hold values from -6 to 6
- routes_a: int32 [4, 1, 1024, 1], P('section', None, 'ep'), may hold values from 0 to 1; in each aligned block of 128 rows (0 to 127, 128 to 255, ..., all dimensions but the last counted through in order) at most 72 rows name the same one
- routes_b: int32 [4, 1, 1024, 1], P('section', None, 'ep'), may hold values from 0 to 1; in each aligned block of 128 rows (0 to 127, 128 to 255, ..., all dimensions but the last counted through in order) at most 72 rows name the same one
- scores_a: float32 [4, 1, 1024, 1], P('section', None, 'ep'), may hold values from 0.5 to 1.5
- scores_b: float32 [4, 1, 1024, 1], P('section', None, 'ep'), may hold values from 0.5 to 1.5
- norm_gain: float32 [4, 3584], P('section'), may hold values from 0.1 to 1.9
- w_gate: bfloat16 [4, 3584, 2048], P('section', None, 'ep'), may hold values from -0.09375 to 0.09375
- w_up: bfloat16 [4, 3584, 2048], P('section', None, 'ep'), may hold values from -0.09375 to 0.09375
- w_down: bfloat16 [4, 2048, 3584], P('section', 'ep'), may hold values from -0.1875 to 0.1875
Outputs:
- out_a: bfloat16 [4, 1024, 3584], P('section', 'ep')
- out_b: bfloat16 [4, 1024, 3584], P('section', 'ep')
Inputs may be any that keep to these rules, and one draw needn't show every extreme that they name: `routes_a`: in each block of 128 rows that one device holds for one layer and step, no expert is named more than 72 times, a bound that some block reaches; a row never names one expert twice. `routes_b`: as for routes_a.
All inputs are finite; a program needn't handle non-finite values.
Results may differ from a plain program's by a relative error of at most 0.0054.
Values may be sent and summed in bfloat16 or wider, within the bound.
A program may use at most 128 MiB of HBM per device.

v0:
```python
import jax
import jax.numpy as jnp
from jax import lax
from jax.sharding import PartitionSpec as P

ES = 4
TOPK = 1
EPSILON = 1e-06


def from_behind(value, axis, steps):
    count = lax.axis_size(axis)
    pairs = [(source, (source + steps) % count) for source in range(count)]
    return lax.ppermute(value, axis, pairs)


def rms_norm(current, gain):
    as_float = current.astype(jnp.float32)
    inverse_rms = lax.rsqrt(jnp.mean(as_float * as_float, axis=-1, keepdims=True) + EPSILON)
    return (as_float * inverse_rms * gain).astype(jnp.bfloat16)


def routing(expert_ids, route_weights, expert_count, capacity):
    token_count, top_count = expert_ids.shape
    flat_ids = expert_ids.reshape(token_count * top_count)
    onehot = (flat_ids[:, None] == jnp.arange(expert_count, dtype=jnp.int32)[None, :]).astype(
        jnp.int32
    )
    before = jnp.cumsum(onehot, axis=0) - onehot
    slot_index = jnp.sum(before * onehot, axis=1)
    column = flat_ids * capacity + slot_index
    placed = column[:, None] == jnp.arange(expert_count * capacity, dtype=jnp.int32)[None, :]
    placed = placed.reshape(token_count, top_count, expert_count * capacity)
    picker = jnp.any(placed, axis=1).astype(jnp.bfloat16)
    mixing = jnp.sum(jnp.where(placed, route_weights[:, :, None], 0.0), axis=1)
    return (picker, mixing)


def prepare(current, expert_ids, route_weights, gain, expert_count, capacity):
    normed = rms_norm(current, gain)
    picker, mixing = routing(expert_ids, route_weights, expert_count, capacity)
    feature_width = normed.shape[1]
    slotted = jnp.einsum("ts,td->sd", picker, normed, preferred_element_type=jnp.float32).astype(
        jnp.bfloat16
    )
    slotted = slotted.reshape(expert_count, 1, capacity, feature_width)
    outgoing = jnp.broadcast_to(slotted, (expert_count, ES, capacity, feature_width))
    return (outgoing.reshape(expert_count * ES, capacity, feature_width), mixing)


def expert_pass(outgoing, gate_cols, up_cols, down_part):
    received = lax.all_to_all(outgoing, "ep", split_axis=0, concat_axis=0, tiled=True)
    source_count, slot_count, feature_width = received.shape
    row_block = received.reshape(source_count * slot_count, feature_width)
    gate_act = jnp.dot(row_block, gate_cols, preferred_element_type=jnp.float32)
    up_act = jnp.dot(row_block, up_cols, preferred_element_type=jnp.float32)
    hidden = (jax.nn.silu(gate_act) * up_act).astype(jnp.bfloat16)
    partial_value = jnp.dot(hidden, down_part, preferred_element_type=jnp.float32).astype(
        jnp.bfloat16
    )
    partial_value = partial_value.reshape(source_count, slot_count, feature_width)
    return lax.all_to_all(partial_value, "ep", split_axis=0, concat_axis=0, tiled=True)


def finish(current, returned, mixing, expert_count):
    feature_width = current.shape[1]
    slot_count = returned.shape[1]
    by_slice = returned.astype(jnp.float32).reshape(expert_count, ES, slot_count, feature_width)
    summed = jnp.sum(by_slice, axis=1).reshape(expert_count * slot_count, feature_width)
    moe_out = jnp.dot(
        mixing, summed, precision=lax.Precision.HIGHEST, preferred_element_type=jnp.float32
    )
    return (current.astype(jnp.float32) + moe_out).astype(jnp.bfloat16)


def on_device(
    flight_a, flight_b, routes_a, routes_b, scores_a, scores_b, norm_gain, w_gate, w_up, w_down
):
    ep_count = lax.axis_size("ep")
    expert_count = ep_count // ES
    tok_dev = flight_a.shape[1]
    capacity = min(tok_dev, 9 * tok_dev * TOPK * ES // (8 * ep_count))
    section_index = lax.axis_index("section")
    last_section = lax.axis_size("section") - 1
    gain = norm_gain[0]
    gate_cols = w_gate[0]
    up_cols = w_up[0]
    down_part = w_down[0]
    current_a = flight_a[0]
    current_b = flight_b[0]
    outgoing_a, mixing_a = prepare(
        current_a, routes_a[0, 0], scores_a[0, 0], gain, expert_count, capacity
    )
    outgoing_b, mixing_b = prepare(
        current_b, routes_b[0, 0], scores_b[0, 0], gain, expert_count, capacity
    )
    returned_a = expert_pass(outgoing_a, gate_cols, up_cols, down_part)
    returned_b = expert_pass(outgoing_b, gate_cols, up_cols, down_part)
    updated_a = finish(current_a, returned_a, mixing_a, expert_count)
    updated_b = finish(current_b, returned_b, mixing_b, expert_count)
    current_a = jnp.where(0 <= section_index, updated_a, current_a)
    current_b = jnp.where(section_index + 0 <= last_section, updated_b, current_b)
    current_a = from_behind(current_a, "section", 1)
    current_b = from_behind(current_b, "section", -1)
    return (current_a[None], current_b[None])


def solution(mesh):
    placed = (
        P("section", "ep", None),
        P("section", "ep", None),
        P("section", None, "ep", None),
        P("section", None, "ep", None),
        P("section", None, "ep", None),
        P("section", None, "ep", None),
        P("section", None),
        P("section", None, "ep"),
        P("section", None, "ep"),
        P("section", "ep", None),
    )
    return jax.shard_map(
        on_device,
        mesh=mesh,
        in_specs=placed,
        out_specs=(P("section", "ep", None), P("section", "ep", None)),
        check_vma=False,
    )
```

profile of v0, /device:TPU:2, one launch (start us, length us, event | category | flops | bytes accessed | tf_op | source)
XLA Modules:
  0.0 256.0 jit_solution(12852984667697311953)
XLA Ops:
  0.6 0.9 fusion.60
  1.5 0.2 reduce_window_sum.18
  1.7 0.8 select_reduce_fusion
  2.5 0.7 multiply_add_fusion
  3.2 1.4 fusion.5
  4.6 0.8 reduce
  5.4 1.7 convolution_convert_fusion.2
  7.1 2.2 broadcast_in_dim.59
  9.3 4.6 %all-to-all-start.2 = ((bf16[8,72,3584]{2,1,0:T(8,128)(2,1)}), bf16[8,72,3584]{2,1,0:T(8,128)(2,1)}, u32[]{:S(2)}, u32[]{:S(2)}) async-start(bf16[8,72,3584]{2,1,0:T(8,128)(2,1)} %bitcast.81), calls=%async_computation.2 | async-start | bytes 8257536 | tf_op jit(solution)/shard_map/all_to_all | solution.py:52
  14.4 0.3 fusion.4
  14.7 1.6 convolution_convert_fusion.3
  16.3 44.4 %all-to-all-done.2 = bf16[8,72,3584]{2,1,0:T(8,128)(2,1)} async-done(((bf16[8,72,3584]{2,1,0:T(8,128)(2,1)}), bf16[8,72,3584]{2,1,0:T(8,128)(2,1)}, u32[]{:S(2)}, u32[]{:S(2)}) %all-to-all-start.2) | async-done | bytes 4128800 | tf_op jit(solution)/shard_map/all_to_all | solution.py:52
  60.7 3.4 %broadcast_in_dim.54 = bf16[2,4,72,3584]{3,2,1,0:T(8,128)(2,1)} broadcast(bf16[2,72,3584]{2,1,0:T(8,128)(2,1)} %bitcast.85), dimensions={0,2,3} | broadcast | bytes 5160960 | tf_op jit(solution)/shard_map/broadcast_in_dim | solution.py:47
  64.1 5.9 %all-to-all-start = ((bf16[8,72,3584]{2,1,0:T(8,128)(2,1)}), bf16[8,72,3584]{2,1,0:T(8,128)(2,1)}, u32[]{:S(2)}, u32[]{:S(2)}) async-start(bf16[8,72,3584]{2,1,0:T(8,128)(2,1)} %bitcast.82), calls=%async_computation | async-start | bytes 8257536 | tf_op jit(solution)/shard_map/all_to_all | solution.py:52
  70.1 4.0 %fusion.12 = f32[576,256]{1,0:T(8,128)S(1)} fusion(bf16[576,3584]{1,0:T(8,128)(2,1)} %bitcast.24, bf16[1,3584,256]{2,1,0:T(8,128)(2,1)} %param.17), kind=kOutput, calls=%fused_computation.22 | convolution fusion | flops 1056964608 | bytes 6553600 | tf_op jit(solution)/shard_map/dot_general | solution.py:55
  74.1 9.1 %convolution_convert_fusion = bf16[576,3584]{1,0:T(8,128)(2,1)} fusion(bf16[1,256,3584]{2,1,0:T(8,128)(2,1)S(1)} %copy-done, bf16[576,3584]{1,0:T(8,128)(2,1)} %bitcast.24, bf16[1,3584,256]{2,1,0:T(8,128)(2,1)} %param.18, f32[576,256]{1,0:T(8,128)S(1)} %fusion.12), kind=kOutput, calls=%fused_computation.2 | convolution fusion | flops 2116878336 | bytes 12517376 | tf_op jit(solution)/shard_map/dot_general | solution.py:58
  83.2 33.9 %all-to-all-done = bf16[8,72,3584]{2,1,0:T(8,128)(2,1)} async-done(((bf16[8,72,3584]{2,1,0:T(8,128)(2,1)}), bf16[8,72,3584]{2,1,0:T(8,128)(2,1)}, u32[]{:S(2)}, u32[]{:S(2)}) %all-to-all-start) | async-done | bytes 4128800 | tf_op jit(solution)/shard_map/all_to_all | solution.py:52
  117.1 6.0 %all-to-all-start.3 = ((bf16[8,72,3584]{2,1,0:T(8,128)(2,1)}), bf16[8,72,3584]{2,1,0:T(8,128)(2,1)}, u32[]{:S(2)}, u32[]{:S(2)}) async-start(bf16[8,72,3584]{2,1,0:T(8,128)(2,1)} %bitcast.88), calls=%async_computation.3 | async-start | bytes 8257536 | tf_op jit(solution)/shard_map/all_to_all | solution.py:62
  123.0 4.0 %fusion.14 = f32[576,256]{1,0:T(8,128)S(1)} fusion(bf16[576,3584]{1,0:T(8,128)(2,1)} %bitcast.8, bf16[1,3584,256]{2,1,0:T(8,128)(2,1)} %param.17), kind=kOutput, calls=%fused_computation.24 | convolution fusion | flops 1056964608 | bytes 6553600 | tf_op jit(solution)/shard_map/dot_general | solution.py:55
  127.0 9.1 %convolution_convert_fusion.1 = bf16[576,3584]{1,0:T(8,128)(2,1)} fusion(bf16[1,256,3584]{2,1,0:T(8,128)(2,1)S(1)} %copy-done, bf16[576,3584]{1,0:T(8,128)(2,1)} %bitcast.8, bf16[1,3584,256]{2,1,0:T(8,128)(2,1)} %param.18, f32[576,256]{1,0:T(8,128)S(1)} %fusion.14), kind=kOutput, calls=%fused_computation.3 | convolution fusion | flops 2116878336 | bytes 12517376 | tf_op jit(solution)/shard_map/dot_general | solution.py:58
  136.1 33.9 %all-to-all-done.3 = bf16[8,72,3584]{2,1,0:T(8,128)(2,1)} async-done(((bf16[8,72,3584]{2,1,0:T(8,128)(2,1)}), bf16[8,72,3584]{2,1,0:T(8,128)(2,1)}, u32[]{:S(2)}, u32[]{:S(2)}) %all-to-all-start.3) | async-done | bytes 4128800 | tf_op jit(solution)/shard_map/all_to_all | solution.py:62
  170.0 5.9 %all-to-all-start.1 = ((bf16[8,72,3584]{2,1,0:T(8,128)(2,1)}), bf16[8,72,3584]{2,1,0:T(8,128)(2,1)}, u32[]{:S(2)}, u32[]{:S(2)}) async-start(bf16[8,72,3584]{2,1,0:T(8,128)(2,1)} %bitcast.87), calls=%async_computation.1 | async-start | bytes 8257536 | tf_op jit(solution)/shard_map/all_to_all | solution.py:62
  176.0 3.1 %convert_reduce_fusion = f32[2,72,3584]{2,1,0:T(8,128)S(1)} fusion(bf16[8,72,3584]{2,1,0:T(8,128)(2,1)} %all-to-all-done.3), kind=kLoop, calls=%fused_computation | loop fusion | flops 3612672 | bytes 6193152 | tf_op jit(solution)/shard_map/reduce_sum | solution.py:69
  179.1 2.8 %fusion.2 = bf16[128,3584]{1,0:T(8,128)(2,1)} fusion(f32[144,3584]{1,0:T(8,128)S(1)} %bitcast.83, bf16[1,128,3584]{2,1,0:T(8,128)(2,1)S(1)} %copy-done.1, pred[]{:T(512)S(6)} %le.3, f32[128]{0:T(128)S(1)} %bitcast.94, s32[128]{0:T(128)S(1)} %multiply_add_fusion), kind=kOutput, calls=%fused_computation.10 | convolution fusion | flops 794595328 | bytes 3900417 | tf_op jit(solution)/shard_map/dot_general | solution.py:70
  182.0 4.3 %collective-permute-start.1 = (bf16[128,3584]{1,0:T(8,128)(2,1)}, bf16[128,3584]{1,0:T(8,128)(2,1)}, u32[]{:S(2)}, u32[]{:S(2)}) collective-permute-start(bf16[128,3584]{1,0:T(8,128)(2,1)} %fusion.2), channel_id=1, source_target_pairs={{0,24},{8,0},{16,8},{24,16},{1,25},{9,1},{17,9},{25,17},{2,26},{10... | collective-permute-start | bytes 2752520 | tf_op jit(solution)/shard_map/ppermute | solution.py:14
  186.3 36.7 %all-to-all-done.1 = bf16[8,72,3584]{2,1,0:T(8,128)(2,1)} async-done(((bf16[8,72,3584]{2,1,0:T(8,128)(2,1)}), bf16[8,72,3584]{2,1,0:T(8,128)(2,1)}, u32[]{:S(2)}, u32[]{:S(2)}) %all-to-all-start.1) | async-done | bytes 4128800 | tf_op jit(solution)/shard_map/all_to_all | solution.py:62
  223.0 3.1 %convert_reduce_fusion.1 = f32[2,72,3584]{2,1,0:T(8,128)S(1)} fusion(bf16[8,72,3584]{2,1,0:T(8,128)(2,1)} %all-to-all-done.1), kind=kLoop, calls=%fused_computation.1 | loop fusion | flops 3612672 | bytes 6193152 | tf_op jit(solution)/shard_map/reduce_sum | solution.py:69
  226.0 1.9 fusion.3
  228.0 2.4 collective-permute-start
  230.3 22.6 %collective-permute-done = bf16[128,3584]{1,0:T(8,128)(2,1)S(1)} collective-permute-done((bf16[128,3584]{1,0:T(8,128)(2,1)S(1)}, bf16[128,3584]{1,0:T(8,128)(2,1)S(1)}, u32[]{:S(2)}, u32[]{:S(2)}) %collective-permute-start) | collective-permute-done | bytes 917536 | tf_op jit(solution)/shard_map/ppermute | solution.py:14
  252.9 0.9 copy.14
  253.9 2.2 copy.15
  (19 shorter events, 0.5 us)
Async XLA Ops:
  0.6 73.4 %copy-start = (bf16[1,256,3584]{2,1,0:T(8,128)(2,1)S(1)}, bf16[1,256,3584]{2,1,0:T(8,128)(2,1)}, u32[]{:S(2)}) copy-start(bf16[1,256,3584]{2,1,0:T(8,128)(2,1)} %param.19) | copy-start | bytes 5505028
  9.3 4.6 %copy-start.3 = (s32[1,1,128,1]{2,3,1,0:T(1,128)S(1)}, s32[1,1,128,1]{2,3,1,0:T(1,128)}, u32[]{:S(2)}) copy-start(s32[1,1,128,1]{2,3,1,0:T(1,128)} %param.12) | copy-start | bytes 1540
  9.3 5.1 %copy-start.2 = (bf16[1,128,3584]{2,1,0:T(8,128)(2,1)S(1)}, bf16[1,128,3584]{2,1,0:T(8,128)(2,1)}, u32[]{:S(2)}) copy-start(bf16[1,128,3584]{2,1,0:T(8,128)(2,1)} %param.10) | copy-start | bytes 2752516
  9.3 51.4 %all-to-all-start.2 = ((bf16[8,72,3584]{2,1,0:T(8,128)(2,1)}), bf16[8,72,3584]{2,1,0:T(8,128)(2,1)}, u32[]{:S(2)}, u32[]{:S(2)}) async-start(bf16[8,72,3584]{2,1,0:T(8,128)(2,1)} %bitcast.81), calls=%async_computation.2 | async-start | bytes 8257536 | tf_op jit(solution)/shard_map/all_to_all | solution.py:52
  64.1 52.9 %all-to-all-start = ((bf16[8,72,3584]{2,1,0:T(8,128)(2,1)}), bf16[8,72,3584]{2,1,0:T(8,128)(2,1)}, u32[]{:S(2)}, u32[]{:S(2)}) async-start(bf16[8,72,3584]{2,1,0:T(8,128)(2,1)} %bitcast.82), calls=%async_computation | async-start | bytes 8257536 | tf_op jit(solution)/shard_map/all_to_all | solution.py:52
  117.1 53.0 %all-to-all-start.3 = ((bf16[8,72,3584]{2,1,0:T(8,128)(2,1)}), bf16[8,72,3584]{2,1,0:T(8,128)(2,1)}, u32[]{:S(2)}, u32[]{:S(2)}) async-start(bf16[8,72,3584]{2,1,0:T(8,128)(2,1)} %bitcast.88), calls=%async_computation.3 | async-start | bytes 8257536 | tf_op jit(solution)/shard_map/all_to_all | solution.py:62
  170.0 52.9 %all-to-all-start.1 = ((bf16[8,72,3584]{2,1,0:T(8,128)(2,1)}), bf16[8,72,3584]{2,1,0:T(8,128)(2,1)}, u32[]{:S(2)}, u32[]{:S(2)}) async-start(bf16[8,72,3584]{2,1,0:T(8,128)(2,1)} %bitcast.87), calls=%async_computation.1 | async-start | bytes 8257536 | tf_op jit(solution)/shard_map/all_to_all | solution.py:62
  176.0 3.1 %copy-start.1 = (bf16[1,128,3584]{2,1,0:T(8,128)(2,1)S(1)}, bf16[1,128,3584]{2,1,0:T(8,128)(2,1)}, u32[]{:S(2)}) copy-start(bf16[1,128,3584]{2,1,0:T(8,128)(2,1)} %param.11) | copy-start | bytes 2752516
  176.0 3.1 %copy-start.4 = (f32[1,1,128,1]{2,3,1,0:T(1,128)S(1)}, f32[1,1,128,1]{2,3,1,0:T(1,128)}, u32[]{:S(2)}) copy-start(f32[1,1,128,1]{2,3,1,0:T(1,128)} %param.15) | copy-start | bytes 1540
  182.0 44.1 %copy-start.5 = (f32[1,1,128,1]{2,3,1,0:T(1,128)S(1)}, f32[1,1,128,1]{2,3,1,0:T(1,128)}, u32[]{:S(2)}) copy-start(f32[1,1,128,1]{2,3,1,0:T(1,128)} %param.14) | copy-start | bytes 1540
  182.0 48.4 %collective-permute-start.1 = (bf16[128,3584]{1,0:T(8,128)(2,1)}, bf16[128,3584]{1,0:T(8,128)(2,1)}, u32[]{:S(2)}, u32[]{:S(2)}) collective-permute-start(bf16[128,3584]{1,0:T(8,128)(2,1)} %fusion.2), channel_id=1, source_target_pairs={{0,24},{8,0},{16,8},{24,16},{1,25},{9,1},{17,9},{25,17},{2,26},{10... | collective-permute-start | bytes 2752520 | tf_op jit(solution)/shard_map/ppermute | solution.py:14
  228.0 25.0 %collective-permute-start = (bf16[128,3584]{1,0:T(8,128)(2,1)S(1)}, bf16[128,3584]{1,0:T(8,128)(2,1)S(1)}, u32[]{:S(2)}, u32[]{:S(2)}) collective-permute-start(bf16[128,3584]{1,0:T(8,128)(2,1)S(1)} %fusion.3), channel_id=1, source_target_pairs={{0,8},{8,16},{16,24},{24,0},{1,9},{9,17},{17,25},{25,1},{2,10},{10... | collective-permute-start | bytes 2752520 | tf_op jit(solution)/shard_map/ppermute | solution.py:14
where the time goes:
time: 257 us; the launch traced here: 256 us
  waiting for transfers between devices  172 us (67%)
  matrix products  34.2 us (13%)
  starting transfers between devices  29.2 us (11%)
  other arithmetic  11.6 us (5%)
  local copies, waits for them, and re-layouts  8.78 us (3%)
    all_to_all x2, waiting for transfers between devices, expert_pass(): lax.all_to_all(outgoing, 'ep', split_axis=0, concat_axis=0, tiled=True)  78.3 us
    all_to_all x2, waiting for transfers between devices, expert_pass(): lax.all_to_all(partial_value, 'ep', split_axis=0, concat_axis=0, tiled=True)  70.6 us
    ppermute x2, waiting for transfers between devices, from_behind(): return lax.ppermute(value, axis, pairs)  22.6 us
    dot_general x2, matrix products, expert_pass(): jnp.dot(hidden, down_part, preferred_element_type=jnp.float32)  18.2 us
    all_to_all x2, starting transfers between devices, expert_pass(): lax.all_to_all(partial_value, 'ep', split_axis=0, concat_axis=0, tiled=True)  11.9 us
    all_to_all x2, starting transfers between devices, expert_pass(): lax.all_to_all(outgoing, 'ep', split_axis=0, concat_axis=0, tiled=True)  10.6 us
    dot_general x2, matrix products, expert_pass(): gate_act = jnp.dot(row_block, gate_cols, preferred_element_type=jnp.float32)  7.95 us
    ppermute x2, starting transfers between devices, from_behind(): return lax.ppermute(value, axis, pairs)  6.69 us
  transfers between devices with their start and end apart: 6, of which 5 were waited for; matrix products, arithmetic and copies ran while one was open for 15% of the time, Pallas kernels for 0%

commit v1 on v0

--- a/solution.py
+++ b/solution.py
@@ -6,6 +6,17 @@
 ES = 4
 TOPK = 1
 EPSILON = 1e-06
+
+
+def in_blocks(x, dim, size):
+    before, after = (x.shape[:dim], x.shape[dim + 1 :])
+    return jnp.moveaxis(x.reshape(*before, size, -1, *after), dim, 0)
+
+
+def laid_out(tiles, dim):
+    shape = list(tiles.shape[1:])
+    shape[dim] *= tiles.shape[0]
+    return jnp.moveaxis(tiles, 0, dim).reshape(shape)
 
 
 def from_behind(value, axis, steps):
@@ -49,7 +60,14 @@
 
 
 def expert_pass(outgoing, gate_cols, up_cols, down_part):
-    received = lax.all_to_all(outgoing, "ep", split_axis=0, concat_axis=0, tiled=True)
+    size, place = (lax.axis_size("ep"), lax.axis_index("ep"))
+    blocks = in_blocks(outgoing, 0, size)
+    outs = [blocks[place]]
+    for step in range(1, size):
+        sent = blocks[place ^ step]
+        outs.append(lax.ppermute(sent, "ep", [(i, i ^ step) for i in range(size)]))
+    blocks = jnp.stack(outs)[place ^ jnp.arange(size)]
+    received = laid_out(blocks, 0)
     source_count, slot_count, feature_width = received.shape
     row_block = received.reshape(source_count * slot_count, feature_width)
     gate_act = jnp.dot(row_block, gate_cols, preferred_element_type=jnp.float32)

time: 257 us -> 263 us (1.023)
  local copies, waits for them, and re-layouts: 8.78 us -> 39 us
  waiting for transfers between devices: 172 us -> 148 us
    ppermute x0 -> x14, waiting for transfers between devices: none -> 87.8 us  [expert_pass(): outs.append(lax.ppermute(sent, 'ep', [(i, i ^ step) for i in range(size)]))]
    all_to_all x2 -> x0, waiting for transfers between devices: 78.3 us -> none  [expert_pass(): lax.all_to_all(outgoing, 'ep', split_axis=0, concat_axis=0, tiled=True)]
    all_to_all x2, waiting for transfers between devices: 70.6 us -> 37.4 us  [expert_pass(): lax.all_to_all(partial_value, 'ep', split_axis=0, concat_axis=0, tiled=True)]
    unnamed x14 -> x32, local copies, waits for them, and re-layouts: 3.11 us -> 23.5 us
    ppermute x0 -> x14, starting transfers between devices: none -> 11.4 us  [expert_pass(): outs.append(lax.ppermute(sent, 'ep', [(i, i ^ step) for i in range(size)]))]
    all_to_all x2 -> x0, starting transfers between devices: 10.6 us -> none  [expert_pass(): lax.all_to_all(outgoing, 'ep', split_axis=0, concat_axis=0, tiled=True)]
    gather x0 -> x2, local copies, waits for them, and re-layouts: none -> 9.79 us  [expert_pass(): blocks = jnp.stack(outs)[place ^ jnp.arange(size)]]
    broadcast_in_dim x2, local copies, waits for them, and re-layouts: 5.67 us -> 0.57 us  [prepare(): jnp.broadcast_to(slotted, (expert_count, ES, capacity, feature_width))]
  transfers between devices with their start and end apart: 6 -> 18, of which waited for: 5 -> 7; matrix products, arithmetic and copies ran while one was open for 15% -> 28% of each run, Pallas kernels for 0% -> 0%
where the time goes in v1:
time: 263 us; the launch traced here: 261 us
  waiting for transfers between devices  148 us (56%)
  local copies, waits for them, and re-layouts  39 us (15%)
  matrix products  33.9 us (13%)
  starting transfers between devices  28.1 us (11%)
  other arithmetic  11.6 us (4%)
    ppermute x14, waiting for transfers between devices, expert_pass(): outs.append(lax.ppermute(sent, 'ep', [(i, i ^ step) for i in range(size)]))  87.8 us
    all_to_all x2, waiting for transfers between devices, expert_pass(): lax.all_to_all(partial_value, 'ep', split_axis=0, concat_axis=0, tiled=True)  37.4 us
    unnamed x32, local copies, waits for them, and re-layouts  23.5 us
    ppermute x2, waiting for transfers between devices, from_behind(): return lax.ppermute(value, axis, pairs)  22.6 us
    dot_general x2, matrix products, expert_pass(): jnp.dot(hidden, down_part, preferred_element_type=jnp.float32)  18.2 us
    ppermute x14, starting transfers between devices, expert_pass(): outs.append(lax.ppermute(sent, 'ep', [(i, i ^ step) for i in range(size)]))  11.4 us
    all_to_all x2, starting transfers between devices, expert_pass(): lax.all_to_all(partial_value, 'ep', split_axis=0, concat_axis=0, tiled=True)  11.4 us
    gather x2, local copies, waits for them, and re-layouts, expert_pass(): blocks = jnp.stack(outs)[place ^ jnp.arange(size)]  9.79 us
  transfers between devices with their start and end apart: 18, of which 7 were waited for; matrix products, arithmetic and copies ran while one was open for 28% of the time, Pallas kernels for 0%

profile of v1, /device:TPU:2, one launch (start us, length us, event | category | flops | bytes accessed | tf_op | source)
XLA Modules:
  0.0 261.5 jit_solution(16318456171257961046)
XLA Ops:
  7.5 2.0 dynamic-slice_bitcast_fusion
  9.5 1.9 collective-permute-start.10
  17.6 1.9 bitcast_dynamic-update-slice_fusion.6
  19.5 4.9 %collective-permute-done.9 = bf16[1,72,3584]{2,1,0:T(8,128)(2,1)} collective-permute-done((bf16[1,72,3584]{2,1,0:T(8,128)(2,1)}, bf16[1,72,3584]{2,1,0:T(8,128)(2,1)}, u32[]{:S(2)}, u32[]{:S(2)}) %collective-permute-start.9) | collective-permute-done | bytes 516128 | tf_op jit(solution)/shard_map/ppermute | solution.py:68
  24.7 1.9 bitcast_dynamic-update-slice_fusion.5
  26.6 8.0 %collective-permute-done.10 = bf16[1,72,3584]{2,1,0:T(8,128)(2,1)} collective-permute-done((bf16[1,72,3584]{2,1,0:T(8,128)(2,1)}, bf16[1,72,3584]{2,1,0:T(8,128)(2,1)}, u32[]{:S(2)}, u32[]{:S(2)}) %collective-permute-start.10) | collective-permute-done | bytes 516128 | tf_op jit(solution)/shard_map/ppermute | solution.py:68
  35.6 1.9 bitcast_dynamic-update-slice_fusion.4
  37.5 1.9 bitcast_dynamic-update-slice_fusion.3
  39.4 18.5 %collective-permute-done.12 = bf16[1,72,3584]{2,1,0:T(8,128)(2,1)} collective-permute-done((bf16[1,72,3584]{2,1,0:T(8,128)(2,1)}, bf16[1,72,3584]{2,1,0:T(8,128)(2,1)}, u32[]{:S(2)}, u32[]{:S(2)}) %collective-permute-start.12) | collective-permute-done | bytes 516128 | tf_op jit(solution)/shard_map/ppermute | solution.py:68
  58.8 1.9 bitcast_dynamic-update-slice_fusion.2
  64.1 4.9 %gather_fusion.1 = bf16[8,72,3584]{2,1,0:T(8,128)(2,1)} fusion(bf16[8,72,3584]{2,1,0:T(8,128)(2,1)} %bitcast.54, s32[1024]{0:T(1024)S(1)} %pad_clamp_fusion), kind=kCustom, calls=%fused_computation.1 | custom fusion | bytes 8257568 | tf_op jit(solution)/shard_map/gather | solution.py:69
  69.0 4.8 %fusion.12 = f32[576,256]{1,0:T(8,128)} fusion(bf16[576,3584]{1,0:T(8,128)(2,1)} %bitcast.152, bf16[1,3584,256]{2,1,0:T(8,128)(2,1)} %param.17), kind=kOutput, calls=%fused_computation.24 | convolution fusion | flops 1056964608 | bytes 6553600 | tf_op jit(solution)/shard_map/dot_general | solution.py:73
  73.8 9.2 %convolution_convert_fusion = bf16[576,3584]{1,0:T(8,128)(2,1)} fusion(bf16[1,256,3584]{2,1,0:T(8,128)(2,1)S(1)} %copy-done, bf16[576,3584]{1,0:T(8,128)(2,1)} %bitcast.153, bf16[1,3584,256]{2,1,0:T(8,128)(2,1)} %param.18, f32[576,256]{1,0:T(8,128)} %fusion.12), kind=kOutput, calls=%fused_computation.4 | convolution fusion | flops 2116878336 | bytes 12517376 | tf_op jit(solution)/shard_map/dot_general | solution.py:76
  83.0 5.9 %all-to-all-start.1 = ((bf16[8,72,3584]{2,1,0:T(8,128)(2,1)}), bf16[8,72,3584]{2,1,0:T(8,128)(2,1)}, u32[]{:S(2)}, u32[]{:S(2)}) async-start(bf16[8,72,3584]{2,1,0:T(8,128)(2,1)} %bitcast.148), calls=%async_computation.1 | async-start | bytes 8257536 | tf_op jit(solution)/shard_map/all_to_all | solution.py:80
  93.2 1.9 bitcast_dynamic-update-slice_fusion.12
  95.0 1.9 bitcast_dynamic-update-slice_fusion.11
  96.9 1.9 bitcast_dynamic-update-slice_fusion.10
  98.8 1.9 bitcast_dynamic-update-slice_fusion.9
  100.6 46.9 %collective-permute-done.5 = bf16[1,72,3584]{2,1,0:T(8,128)(2,1)S(1)} collective-permute-done((bf16[1,72,3584]{2,1,0:T(8,128)(2,1)S(1)}, bf16[1,72,3584]{2,1,0:T(8,128)(2,1)S(1)}, u32[]{:S(2)}, u32[]{:S(2)}) %collective-permute-start.5) | collective-permute-done | bytes 516128 | tf_op jit(solution)/shard_map/ppermute | solution.py:68
  148.4 9.5 %collective-permute-done.6 = bf16[1,72,3584]{2,1,0:T(8,128)(2,1)S(1)} collective-permute-done((bf16[1,72,3584]{2,1,0:T(8,128)(2,1)S(1)}, bf16[1,72,3584]{2,1,0:T(8,128)(2,1)S(1)}, u32[]{:S(2)}, u32[]{:S(2)}) %collective-permute-start.6) | collective-permute-done | bytes 516128 | tf_op jit(solution)/shard_map/ppermute | solution.py:68
  158.7 4.9 %gather_fusion = bf16[8,72,3584]{2,1,0:T(8,128)(2,1)} fusion(bf16[8,72,3584]{2,1,0:T(8,128)(2,1)} %bitcast.145, s32[1024]{0:T(1024)S(1)} %pad_clamp_fusion), kind=kCustom, calls=%fused_computation | custom fusion | bytes 8257568 | tf_op jit(solution)/shard_map/gather | solution.py:69
  163.6 4.0 %fusion.14 = f32[576,256]{1,0:T(8,128)S(1)} fusion(bf16[576,3584]{1,0:T(8,128)(2,1)} %bitcast.150, bf16[1,3584,256]{2,1,0:T(8,128)(2,1)} %param.17), kind=kOutput, calls=%fused_computation.26 | convolution fusion | flops 1056964608 | bytes 6553600 | tf_op jit(solution)/shard_map/dot_general | solution.py:73
  167.6 9.1 %convolution_convert_fusion.1 = bf16[576,3584]{1,0:T(8,128)(2,1)} fusion(bf16[1,256,3584]{2,1,0:T(8,128)(2,1)S(1)} %copy-done, bf16[576,3584]{1,0:T(8,128)(2,1)} %bitcast.151, bf16[1,3584,256]{2,1,0:T(8,128)(2,1)} %param.18, f32[576,256]{1,0:T(8,128)S(1)} %fusion.14), kind=kOutput, calls=%fused_computation.5 | convolution fusion | flops 2116878336 | bytes 12517376 | tf_op jit(solution)/shard_map/dot_general | solution.py:76
  176.6 5.5 %all-to-all-start = ((bf16[8,72,3584]{2,1,0:T(8,128)(2,1)}), bf16[8,72,3584]{2,1,0:T(8,128)(2,1)}, u32[]{:S(2)}, u32[]{:S(2)}) async-start(bf16[8,72,3584]{2,1,0:T(8,128)(2,1)} %bitcast.149), calls=%async_computation | async-start | bytes 8257536 | tf_op jit(solution)/shard_map/all_to_all | solution.py:80
  182.2 3.1 %convert_reduce_fusion = f32[2,72,3584]{2,1,0:T(8,128)S(1)} fusion(bf16[8,72,3584]{2,1,0:T(8,128)(2,1)} %all-to-all-done.1), kind=kLoop, calls=%fused_computation.2 | loop fusion | flops 3612672 | bytes 6193152 | tf_op jit(solution)/shard_map/reduce_sum | solution.py:87
  185.3 2.8 %fusion.2 = bf16[128,3584]{1,0:T(8,128)(2,1)} fusion(f32[144,3584]{1,0:T(8,128)S(1)} %bitcast.143, bf16[1,128,3584]{2,1,0:T(8,128)(2,1)S(1)} %copy-done.1, pred[]{:T(512)S(6)} %le.3, f32[128]{0:T(128)S(1)} %bitcast.159, s32[128]{0:T(128)S(1)} %multiply_add_fusion), kind=kOutput, calls=%fused_computation.12 | convolution fusion | flops 794595328 | bytes 3900417 | tf_op jit(solution)/shard_map/dot_general | solution.py:88
  188.1 3.6 %collective-permute-start.15 = (bf16[128,3584]{1,0:T(8,128)(2,1)}, bf16[128,3584]{1,0:T(8,128)(2,1)}, u32[]{:S(2)}, u32[]{:S(2)}) collective-permute-start(bf16[128,3584]{1,0:T(8,128)(2,1)} %fusion.2), channel_id=1, source_target_pairs={{0,24},{8,0},{16,8},{24,16},{1,25},{9,1},{17,9},{25,17},{2,26},{10... | collective-permute-start | bytes 2752520 | tf_op jit(solution)/shard_map/ppermute | solution.py:25
  191.7 37.4 %all-to-all-done = bf16[8,72,3584]{2,1,0:T(8,128)(2,1)} async-done(((bf16[8,72,3584]{2,1,0:T(8,128)(2,1)}), bf16[8,72,3584]{2,1,0:T(8,128)(2,1)}, u32[]{:S(2)}, u32[]{:S(2)}) %all-to-all-start) | async-done | bytes 4128800 | tf_op jit(solution)/shard_map/all_to_all | solution.py:80
  229.2 3.1 %convert_reduce_fusion.1 = f32[2,72,3584]{2,1,0:T(8,128)S(1)} fusion(bf16[8,72,3584]{2,1,0:T(8,128)(2,1)} %all-to-all-done), kind=kLoop, calls=%fused_computation.3 | loop fusion | flops 3612672 | bytes 6193152 | tf_op jit(solution)/shard_map/reduce_sum | solution.py:87
  232.2 1.9 fusion.3
  235.8 22.6 %collective-permute-done.7 = bf16[128,3584]{1,0:T(8,128)(2,1)S(1)} collective-permute-done((bf16[128,3584]{1,0:T(8,128)(2,1)S(1)}, bf16[128,3584]{1,0:T(8,128)(2,1)S(1)}, u32[]{:S(2)}, u32[]{:S(2)}) %collective-permute-start.7) | collective-permute-done | bytes 917536 | tf_op jit(solution)/shard_map/ppermute | solution.py:25
  259.3 2.2 copy.29
  (69 shorter events, 27.1 us)
Async XLA Ops:
  0.6 73.2 %copy-start = (bf16[1,256,3584]{2,1,0:T(8,128)(2,1)S(1)}, bf16[1,256,3584]{2,1,0:T(8,128)(2,1)}, u32[]{:S(2)}) copy-start(bf16[1,256,3584]{2,1,0:T(8,128)(2,1)} %param.19) | copy-start | bytes 5505028
  7.5 5.6 %copy-start.6 = (s32[1,1,128,1]{2,3,1,0:T(1,128)S(1)}, s32[1,1,128,1]{2,3,1,0:T(1,128)}, u32[]{:S(2)}) copy-start(s32[1,1,128,1]{2,3,1,0:T(1,128)} %param.12) | copy-start | bytes 1540
  7.5 6.0 %copy-start.2 = (bf16[1,128,3584]{2,1,0:T(8,128)(2,1)S(1)}, bf16[1,128,3584]{2,1,0:T(8,128)(2,1)}, u32[]{:S(2)}) copy-start(bf16[1,128,3584]{2,1,0:T(8,128)(2,1)} %param.10) | copy-start | bytes 2752516
  9.5 6.6 %collective-permute-start.8 = (bf16[1,72,3584]{2,1,0:T(8,128)(2,1)}, bf16[1,72,3584]{2,1,0:T(8,128)(2,1)}, u32[]{:S(2)}, u32[]{:S(2)}) collective-permute-start(bf16[1,72,3584]{2,1,0:T(8,128)(2,1)} %get-tuple-element.8), channel_id=1, source_target_pairs={{0,1},{1,0},{2,3},{3,2},{4,5},{5,4},{6,7},{7,6},{8,9},{9,8},{10,11... | collective-permute-start | bytes 1548296 | tf_op jit(solution)/shard_map/ppermute | solution.py:68
  9.5 14.9 %collective-permute-start.9 = (bf16[1,72,3584]{2,1,0:T(8,128)(2,1)}, bf16[1,72,3584]{2,1,0:T(8,128)(2,1)}, u32[]{:S(2)}, u32[]{:S(2)}) collective-permute-start(bf16[1,72,3584]{2,1,0:T(8,128)(2,1)} %get-tuple-element.7), channel_id=1, source_target_pairs={{0,2},{1,3},{2,0},{3,1},{4,6},{5,7},{6,4},{7,5},{8,10},{9,11},{10,... | collective-permute-start | bytes 1548296 | tf_op jit(solution)/shard_map/ppermute | solution.py:68
  9.5 25.1 %collective-permute-start.10 = (bf16[1,72,3584]{2,1,0:T(8,128)(2,1)}, bf16[1,72,3584]{2,1,0:T(8,128)(2,1)}, u32[]{:S(2)}, u32[]{:S(2)}) collective-permute-start(bf16[1,72,3584]{2,1,0:T(8,128)(2,1)} %get-tuple-element.6), channel_id=1, source_target_pairs={{0,3},{1,2},{2,1},{3,0},{4,7},{5,6},{6,5},{7,4},{8,11},{9,10},{10,... | collective-permute-start | bytes 1548296 | tf_op jit(solution)/shard_map/ppermute | solution.py:68
  11.4 26.1 %collective-permute-start.11 = (bf16[1,72,3584]{2,1,0:T(8,128)(2,1)}, bf16[1,72,3584]{2,1,0:T(8,128)(2,1)}, u32[]{:S(2)}, u32[]{:S(2)}) collective-permute-start(bf16[1,72,3584]{2,1,0:T(8,128)(2,1)} %get-tuple-element.5), channel_id=1, source_target_pairs={{0,4},{1,5},{2,6},{3,7},{4,0},{5,1},{6,2},{7,3},{8,12},{9,13},{10,... | collective-permute-start | bytes 1548296 | tf_op jit(solution)/shard_map/ppermute | solution.py:68
  12.9 45.0 %collective-permute-start.12 = (bf16[1,72,3584]{2,1,0:T(8,128)(2,1)}, bf16[1,72,3584]{2,1,0:T(8,128)(2,1)}, u32[]{:S(2)}, u32[]{:S(2)}) collective-permute-start(bf16[1,72,3584]{2,1,0:T(8,128)(2,1)} %get-tuple-element.4), channel_id=1, source_target_pairs={{0,5},{1,4},{2,7},{3,6},{4,1},{5,0},{6,3},{7,2},{8,13},{9,12},{10,... | collective-permute-start | bytes 1548296 | tf_op jit(solution)/shard_map/ppermute | solution.py:68
  14.6 1.5 copy-start.5
  14.6 9.9 %copy-start.4 = (bf16[1,72,3584]{2,1,0:T(8,128)(2,1)S(1)}, bf16[1,72,3584]{2,1,0:T(8,128)(2,1)}, u32[]{:S(2)}) copy-start(bf16[1,72,3584]{2,1,0:T(8,128)(2,1)} %get-tuple-element.2) | copy-start | bytes 1548292
  16.1 44.5 %collective-permute-start.13 = (bf16[1,72,3584]{2,1,0:T(8,128)(2,1)S(1)}, bf16[1,72,3584]{2,1,0:T(8,128)(2,1)S(1)}, u32[]{:S(2)}, u32[]{:S(2)}) collective-permute-start(bf16[1,72,3584]{2,1,0:T(8,128)(2,1)S(1)} %copy-done.5), channel_id=1, source_target_pairs={{0,6},{1,7},{2,4},{3,5},{4,2},{5,3},{6,0},{7,1},{8,14},{9,15},{10,... | collective-permute-start | bytes 1548296 | tf_op jit(solution)/shard_map/ppermute | solution.py:68
  24.5 38.8 %collective-permute-start.14 = (bf16[1,72,3584]{2,1,0:T(8,128)(2,1)S(1)}, bf16[1,72,3584]{2,1,0:T(8,128)(2,1)S(1)}, u32[]{:S(2)}, u32[]{:S(2)}) collective-permute-start(bf16[1,72,3584]{2,1,0:T(8,128)(2,1)S(1)} %copy-done.4), channel_id=1, source_target_pairs={{0,7},{1,6},{2,5},{3,4},{4,3},{5,2},{6,1},{7,0},{8,15},{9,14},{10,... | collective-permute-start | bytes 1548296 | tf_op jit(solution)/shard_map/ppermute | solution.py:68
  34.6 54.3 %collective-permute-start = (bf16[1,72,3584]{2,1,0:T(8,128)(2,1)}, bf16[1,72,3584]{2,1,0:T(8,128)(2,1)}, u32[]{:S(2)}, u32[]{:S(2)}) collective-permute-start(bf16[1,72,3584]{2,1,0:T(8,128)(2,1)} %get-tuple-element.16), channel_id=1, source_target_pairs={{0,1},{1,0},{2,3},{3,2},{4,5},{5,4},{6,7},{7,6},{8,9},{9,8},{10,11... | collective-permute-start | bytes 1548296 | tf_op jit(solution)/shard_map/ppermute | solution.py:68
  37.5 54.8 %collective-permute-start.1 = (bf16[1,72,3584]{2,1,0:T(8,128)(2,1)}, bf16[1,72,3584]{2,1,0:T(8,128)(2,1)}, u32[]{:S(2)}, u32[]{:S(2)}) collective-permute-start(bf16[1,72,3584]{2,1,0:T(8,128)(2,1)} %get-tuple-element.15), channel_id=1, source_target_pairs={{0,2},{1,3},{2,0},{3,1},{4,6},{5,7},{6,4},{7,5},{8,10},{9,11},{10,... | collective-permute-start | bytes 1548296 | tf_op jit(solution)/shard_map/ppermute | solution.py:68
  57.8 37.2 %collective-permute-start.2 = (bf16[1,72,3584]{2,1,0:T(8,128)(2,1)}, bf16[1,72,3584]{2,1,0:T(8,128)(2,1)}, u32[]{:S(2)}, u32[]{:S(2)}) collective-permute-start(bf16[1,72,3584]{2,1,0:T(8,128)(2,1)} %get-tuple-element.14), channel_id=1, source_target_pairs={{0,3},{1,2},{2,1},{3,0},{4,7},{5,6},{6,5},{7,4},{8,11},{9,10},{10,... | collective-permute-start | bytes 1548296 | tf_op jit(solution)/shard_map/ppermute | solution.py:68
  60.7 36.2 %collective-permute-start.3 = (bf16[1,72,3584]{2,1,0:T(8,128)(2,1)}, bf16[1,72,3584]{2,1,0:T(8,128)(2,1)}, u32[]{:S(2)}, u32[]{:S(2)}) collective-permute-start(bf16[1,72,3584]{2,1,0:T(8,128)(2,1)} %get-tuple-element.13), channel_id=1, source_target_pairs={{0,4},{1,5},{2,6},{3,7},{4,0},{5,1},{6,2},{7,3},{8,12},{9,13},{10,... | collective-permute-start | bytes 1548296 | tf_op jit(solution)/shard_map/ppermute | solution.py:68
  63.3 35.5 %collective-permute-start.4 = (bf16[1,72,3584]{2,1,0:T(8,128)(2,1)S(1)}, bf16[1,72,3584]{2,1,0:T(8,128)(2,1)}, u32[]{:S(2)}, u32[]{:S(2)}) collective-permute-start(bf16[1,72,3584]{2,1,0:T(8,128)(2,1)S(1)} %get-tuple-element.12), channel_id=1, source_target_pairs={{0,5},{1,4},{2,7},{3,6},{4,1},{5,0},{6,3},{7,2},{8,13},{9,12},{10,... | collective-permute-start | bytes 1548296 | tf_op jit(solution)/shard_map/ppermute | solution.py:68
  83.0 93.6 %all-to-all-start.1 = ((bf16[8,72,3584]{2,1,0:T(8,128)(2,1)}), bf16[8,72,3584]{2,1,0:T(8,128)(2,1)}, u32[]{:S(2)}, u32[]{:S(2)}) async-start(bf16[8,72,3584]{2,1,0:T(8,128)(2,1)} %bitcast.148), calls=%async_computation.1 | async-start | bytes 8257536 | tf_op jit(solution)/shard_map/all_to_all | solution.py:80
  88.9 58.6 %collective-permute-start.5 = (bf16[1,72,3584]{2,1,0:T(8,128)(2,1)S(1)}, bf16[1,72,3584]{2,1,0:T(8,128)(2,1)S(1)}, u32[]{:S(2)}, u32[]{:S(2)}) collective-permute-start(bf16[1,72,3584]{2,1,0:T(8,128)(2,1)S(1)} %get-tuple-element.11), channel_id=1, source_target_pairs={{0,6},{1,7},{2,4},{3,5},{4,2},{5,3},{6,0},{7,1},{8,14},{9,15},{10,... | collective-permute-start | bytes 1548296 | tf_op jit(solution)/shard_map/ppermute | solution.py:68
  92.3 65.6 %collective-permute-start.6 = (bf16[1,72,3584]{2,1,0:T(8,128)(2,1)S(1)}, bf16[1,72,3584]{2,1,0:T(8,128)(2,1)S(1)}, u32[]{:S(2)}, u32[]{:S(2)}) collective-permute-start(bf16[1,72,3584]{2,1,0:T(8,128)(2,1)S(1)} %get-tuple-element.10), channel_id=1, source_target_pairs={{0,7},{1,6},{2,5},{3,4},{4,3},{5,2},{6,1},{7,0},{8,15},{9,14},{10,... | collective-permute-start | bytes 1548296 | tf_op jit(solution)/shard_map/ppermute | solution.py:68
  176.6 52.5 %all-to-all-start = ((bf16[8,72,3584]{2,1,0:T(8,128)(2,1)}), bf16[8,72,3584]{2,1,0:T(8,128)(2,1)}, u32[]{:S(2)}, u32[]{:S(2)}) async-start(bf16[8,72,3584]{2,1,0:T(8,128)(2,1)} %bitcast.149), calls=%async_computation | async-start | bytes 8257536 | tf_op jit(solution)/shard_map/all_to_all | solution.py:80
  182.2 3.1 %copy-start.1 = (bf16[1,128,3584]{2,1,0:T(8,128)(2,1)S(1)}, bf16[1,128,3584]{2,1,0:T(8,128)(2,1)}, u32[]{:S(2)}) copy-start(bf16[1,128,3584]{2,1,0:T(8,128)(2,1)} %param.11) | copy-start | bytes 2752516
  182.2 3.1 %copy-start.7 = (f32[1,1,128,1]{2,3,1,0:T(1,128)S(1)}, f32[1,1,128,1]{2,3,1,0:T(1,128)}, u32[]{:S(2)}) copy-start(f32[1,1,128,1]{2,3,1,0:T(1,128)} %param.15) | copy-start | bytes 1540
  185.3 46.9 %copy-start.8 = (f32[1,1,128,1]{2,3,1,0:T(1,128)S(1)}, f32[1,1,128,1]{2,3,1,0:T(1,128)}, u32[]{:S(2)}) copy-start(f32[1,1,128,1]{2,3,1,0:T(1,128)} %param.14) | copy-start | bytes 1540
  188.1 44.1 %copy-start.3 = (bf16[1,128,3584]{2,1,0:T(8,128)(2,1)S(1)}, bf16[1,128,3584]{2,1,0:T(8,128)(2,1)}, u32[]{:S(2)}) copy-start(bf16[1,128,3584]{2,1,0:T(8,128)(2,1)} %param.10) | copy-start | bytes 2752516
  188.1 47.7 %collective-permute-start.15 = (bf16[128,3584]{1,0:T(8,128)(2,1)}, bf16[128,3584]{1,0:T(8,128)(2,1)}, u32[]{:S(2)}, u32[]{:S(2)}) collective-permute-start(bf16[128,3584]{1,0:T(8,128)(2,1)} %fusion.2), channel_id=1, source_target_pairs={{0,24},{8,0},{16,8},{24,16},{1,25},{9,1},{17,9},{25,17},{2,26},{10... | collective-permute-start | bytes 2752520 | tf_op jit(solution)/shard_map/ppermute | solution.py:25
  234.2 24.2 %collective-permute-start.7 = (bf16[128,3584]{1,0:T(8,128)(2,1)S(1)}, bf16[128,3584]{1,0:T(8,128)(2,1)S(1)}, u32[]{:S(2)}, u32[]{:S(2)}) collective-permute-start(bf16[128,3584]{1,0:T(8,128)(2,1)S(1)} %fusion.3), channel_id=1, source_target_pairs={{0,8},{8,16},{16,24},{24,0},{1,9},{9,17},{17,25},{25,1},{2,10},{10... | collective-permute-start | bytes 2752520 | tf_op jit(solution)/shard_map/ppermute | solution.py:25
